TPU v7x, 256 devices: a whole 4x4x8 slice. The times are simulated.
256 devices in a mesh: ctx: 8 (over x_hi, y), ep: 32 (over z, x_lo, core).
Axes of the slice: x: 4 (x_hi: 2, x_lo: 2; x = x_hi * 2 + x_lo), y: 4, z: 8, core: 2. Of those that a mesh axis runs over, the one named last changes fastest.
Arguments:
- queries: bfloat16 [32, 1024, 2048], P('ep', 'ctx'), may hold values from -28 to 28
- keys: bfloat16 [32, 1024, 256], P('ep', 'ctx'), may hold values from -6 to 6
- values: bfloat16 [32, 1024, 256], P('ep', 'ctx'), may hold values from -6 to 6
- docs: int32 [32, 1024], P('ep', 'ctx'), may hold values from 0 to 2, as said below
- resid: bfloat16 [32, 1024, 2048], P('ep', 'ctx'), may hold values from -6 to 6
- norm_gain: float32 [2048], replicated, may hold values from 0.25 to 1.75
- routes: int32 [32, 1024, 4], P('ep', 'ctx'), may hold values from 0 to 31, all different within a row; in each aligned block of 128 rows (0 to 127, 128 to 255, ..., all dimensions but the last counted through in order) at most 20 rows name the same one
- gates: float32 [32, 1024, 4], P('ep', 'ctx'), may hold values from 0.1 to 1
- w_gate: bfloat16 [32, 2048, 384], P('ep', 'ctx'), may hold values from -0.125 to 0.125
- w_up: bfloat16 [32, 2048, 384], P('ep', 'ctx'), may hold values from -0.125 to 0.125
- w_down: bfloat16 [32, 2048, 384], P('ep', 'ctx'), may hold values from -0.3125 to 0.3125
- grad_out: bfloat16 [32, 1024, 2048], P('ep', 'ctx'), may hold values from -6 to 6
Outputs:
- block_out: bfloat16 [32, 1024, 2048], P('ep', 'ctx')
- query_grad: bfloat16 [32, 1024, 2048], P('ep', 'ctx')
- key_grad: bfloat16 [32, 1024, 256], P('ep', 'ctx')
- value_grad: bfloat16 [32, 1024, 256], P('ep', 'ctx')
- resid_grad: bfloat16 [32, 1024, 2048], P('ep', 'ctx')
- gate_grad: float32 [32, 1024, 4], P('ep', 'ctx')
- w_gate_grad: bfloat16 [32, 2048, 384], P('ep', 'ctx')
- w_up_grad: bfloat16 [32, 2048, 384], P('ep', 'ctx')
- w_down_grad: bfloat16 [32, 2048, 384], P('ep', 'ctx')
Inputs may be any that keep to these rules, and one draw needn't show every extreme that they name: `docs`: each sequence holds exactly three documents, ids 0, 1 and 2, each a run of one or more positions, in this order. `routes`: the 4 entries of a token name different experts. Among the tokens of one device (the aligned blocks of 128 positions of a sequence), no expert is named more than 20 times, a bound that some block reaches.
All inputs are finite; a program needn't handle non-finite values.
Results may differ from a plain program's by a relative error of at most 0.04.
Values may be sent and summed in bfloat16 or wider, within the bound.
A program may use at most 128 MiB of HBM per device.

v0:
```python
import jax
import jax.numpy as jnp
from jax import lax
from jax.sharding import PartitionSpec as P

HD = 128


def attention_probs(query_rows, key_rows, query_docs, key_docs, query_start):
    count = query_rows.shape[0]
    total = key_rows.shape[0]
    heads_kv = key_rows.shape[1] // HD
    grouped = query_rows.reshape(count, heads_kv, -1, HD)
    keyed = key_rows.reshape(total, heads_kv, HD)
    query_places = query_start + jnp.arange(count)
    key_places = jnp.arange(total)
    allowed = (query_docs[:, None] == key_docs[None, :]) & (
        key_places[None, :] <= query_places[:, None]
    )
    offset = jnp.where(allowed, 0.0, -1e30).astype(jnp.float32)
    scores = (
        jnp.einsum("ikgd,jkd->kgij", grouped, keyed, preferred_element_type=jnp.float32)
        * float(HD) ** (-0.5)
        + offset
    )
    highest = jnp.max(scores, axis=-1, keepdims=True)
    raised = jnp.exp(scores - highest)
    return raised / jnp.sum(raised, axis=-1, keepdims=True)


def route_rows(rows, n_ep):
    return lax.all_to_all(
        rows.reshape(n_ep, -1, rows.shape[-1]), "ep", split_axis=0, concat_axis=0, tiled=True
    )


def per_device(
    queries, keys, values, docs, resid, norm_gain, routes, gates, w_gate, w_up, w_down, grad_out
):
    tok_rows = queries.shape[1]
    width = resid.shape[2]
    n_ep = lax.axis_size("ep")
    exp_dev = w_gate.shape[0]
    hidden_units = w_gate.shape[2]
    top_count = routes.shape[2]
    experts_all = exp_dev * n_ep
    capacity = max(2, (5 * tok_rows * top_count + 4 * experts_all - 1) // (4 * experts_all))
    query_start = lax.axis_index("ctx") * tok_rows
    score_scale = float(HD) ** (-0.5)
    query_rows = queries[0]
    query_docs = docs[0]
    all_keys, all_values, all_docs = (
        lax.all_gather(keys[0], "ctx", axis=0, tiled=True),
        lax.all_gather(values[0], "ctx", axis=0, tiled=True),
        lax.all_gather(docs[0], "ctx", axis=0, tiled=True),
    )
    total = all_keys.shape[0]
    heads_kv = all_keys.shape[1] // HD
    probs = attention_probs(query_rows, all_keys, query_docs, all_docs, query_start)
    probs_b = probs.astype(jnp.bfloat16)
    value_heads = all_values.reshape(total, heads_kv, HD)
    attn = jnp.einsum("kgij,jkd->ikgd", probs_b, value_heads, preferred_element_type=jnp.float32)
    attn = attn.reshape(tok_rows, width).astype(jnp.bfloat16)
    hidden_f = (
        (resid[0].astype(jnp.float32) + attn.astype(jnp.float32))
        .astype(jnp.bfloat16)
        .astype(jnp.float32)
    )
    rstd = lax.rsqrt(jnp.mean(hidden_f * hidden_f, axis=-1, keepdims=True) + 1e-06)
    normed = (hidden_f * rstd * norm_gain).astype(jnp.bfloat16)
    flat_routes = routes[0].reshape(tok_rows * top_count)
    onehot = (flat_routes[:, None] == jnp.arange(experts_all, dtype=jnp.int32)[None, :]).astype(
        jnp.int32
    )
    ranks = jnp.cumsum(onehot, axis=0) - onehot
    slots = jnp.sum(ranks * onehot, axis=-1)
    targets = flat_routes * capacity + slots
    repeated = jnp.repeat(normed, top_count, axis=0)
    outgoing = jnp.zeros((experts_all * capacity, width), jnp.bfloat16).at[targets].set(repeated)
    upstream = grad_out[0]
    upstream_rep = jnp.repeat(upstream, top_count, axis=0).astype(jnp.float32)
    gate_flat = gates[0].reshape(tok_rows * top_count)
    d_out_rows = (gate_flat[:, None] * upstream_rep).astype(jnp.bfloat16)
    outgoing_grad = (
        jnp.zeros((experts_all * capacity, width), jnp.bfloat16).at[targets].set(d_out_rows)
    )
    received = route_rows(outgoing, n_ep).reshape(n_ep, exp_dev, capacity, width)
    gate_full, up_full, down_full = (
        lax.all_gather(w_gate, "ctx", axis=1, tiled=True),
        lax.all_gather(w_up, "ctx", axis=1, tiled=True),
        lax.all_gather(w_down, "ctx", axis=1, tiled=True),
    )
    pre_gate = jnp.einsum("slcd,ldf->slcf", received, gate_full, preferred_element_type=jnp.float32)
    pre_up = jnp.einsum("slcd,ldf->slcf", received, up_full, preferred_element_type=jnp.float32)
    sigma = jax.nn.sigmoid(pre_gate)
    silu_val = pre_gate * sigma
    activ = (silu_val * pre_up).astype(jnp.bfloat16)
    expert_out = jnp.einsum(
        "slcf,ldf->slcd", activ, down_full, preferred_element_type=jnp.float32
    ).astype(jnp.bfloat16)
    returned = route_rows(expert_out, n_ep).reshape(experts_all * capacity, width)
    d_out = route_rows(outgoing_grad, n_ep).reshape(n_ep, exp_dev, capacity, width)
    d_activ = jnp.einsum("slcd,ldf->slcf", d_out, down_full, preferred_element_type=jnp.float32)
    d_gate = (d_activ * pre_up * sigma * (1.0 + pre_gate * (1.0 - sigma))).astype(jnp.bfloat16)
    d_up = (d_activ * silu_val).astype(jnp.bfloat16)
    d_row = (
        jnp.einsum("slcf,ldf->slcd", d_gate, gate_full, preferred_element_type=jnp.float32)
        + jnp.einsum("slcf,ldf->slcd", d_up, up_full, preferred_element_type=jnp.float32)
    ).astype(jnp.bfloat16)
    shard_rows = w_gate.shape[1]
    gate_term = jnp.einsum("slcd,slcf->dlf", received, d_gate, preferred_element_type=jnp.float32)
    up_term = jnp.einsum("slcd,slcf->dlf", received, d_up, preferred_element_type=jnp.float32)
    down_term = jnp.einsum("slcd,slcf->dlf", d_out, activ, preferred_element_type=jnp.float32)
    summed = lax.psum_scatter(
        jnp.stack([gate_term, up_term, down_term], axis=1)
        .reshape(shard_rows * lax.axis_size("ctx"), 3 * exp_dev * hidden_units)
        .astype(jnp.bfloat16),
        "ctx",
        scatter_dimension=0,
        tiled=True,
    ).astype(jnp.float32)
    summed = (
        summed.reshape(shard_rows, 3, exp_dev, hidden_units)
        .transpose(1, 2, 0, 3)
        .astype(jnp.bfloat16)
    )
    back_rows = route_rows(d_row, n_ep).reshape(experts_all * capacity, width)
    own_out = returned[targets].astype(jnp.float32)
    moe_sum = jnp.sum((gate_flat[:, None] * own_out).reshape(tok_rows, top_count, width), axis=1)
    block_out = (hidden_f + moe_sum).astype(jnp.bfloat16)
    gate_grad = jnp.sum(upstream_rep * own_out, axis=-1).reshape(tok_rows, top_count)
    d_normed = jnp.sum(
        back_rows[targets].astype(jnp.float32).reshape(tok_rows, top_count, width), axis=1
    )
    scaled = norm_gain * d_normed
    resid_grad = (
        upstream.astype(jnp.float32)
        + rstd * scaled
        - hidden_f * rstd**3 * jnp.mean(scaled * hidden_f, axis=-1, keepdims=True)
    )
    resid_grad = resid_grad.astype(jnp.bfloat16)
    grad_heads = resid_grad.reshape(tok_rows, heads_kv, -1, HD)
    attn_heads = attn.reshape(tok_rows, heads_kv, -1, HD)
    delta = jnp.einsum("ikgd,ikgd->kgi", grad_heads, attn_heads, preferred_element_type=jnp.float32)
    d_probs = jnp.einsum(
        "ikgd,jkd->kgij", grad_heads, value_heads, preferred_element_type=jnp.float32
    )
    d_scores = (probs * (d_probs - delta[..., None])).astype(jnp.bfloat16)
    key_heads = all_keys.reshape(total, heads_kv, HD)
    query_heads = query_rows.reshape(tok_rows, heads_kv, -1, HD)
    query_grad = (
        jnp.einsum("kgij,jkd->ikgd", d_scores, key_heads, preferred_element_type=jnp.float32)
        * score_scale
    )
    query_grad = query_grad.reshape(tok_rows, width).astype(jnp.bfloat16)
    key_terms = (
        jnp.einsum("kgij,ikgd->jkd", d_scores, query_heads, preferred_element_type=jnp.float32)
        * score_scale
    )
    value_terms = jnp.einsum(
        "kgij,ikgd->jkd", probs_b, grad_heads, preferred_element_type=jnp.float32
    )
    kv_terms = jnp.concatenate(
        [key_terms.reshape(total, heads_kv * HD), value_terms.reshape(total, heads_kv * HD)], axis=1
    )
    kv_grads = lax.psum_scatter(
        kv_terms.astype(jnp.bfloat16), "ctx", scatter_dimension=0, tiled=True
    ).astype(jnp.float32)
    key_grad = kv_grads[:, : heads_kv * HD].astype(jnp.bfloat16)
    value_grad = kv_grads[:, heads_kv * HD :].astype(jnp.bfloat16)
    return (
        block_out[None],
        query_grad[None],
        key_grad[None],
        value_grad[None],
        resid_grad[None],
        gate_grad[None],
        summed[0],
        summed[1],
        summed[2],
    )


def solution(mesh):
    return jax.shard_map(
        per_device,
        mesh=mesh,
        in_specs=(
            P("ep", "ctx", None),
            P("ep", "ctx", None),
            P("ep", "ctx", None),
            P("ep", "ctx"),
            P("ep", "ctx", None),
            P(),
            P("ep", "ctx", None),
            P("ep", "ctx", None),
            P("ep", "ctx", None),
            P("ep", "ctx", None),
            P("ep", "ctx", None),
            P("ep", "ctx", None),
        ),
        out_specs=(
            P("ep", "ctx", None),
            P("ep", "ctx", None),
            P("ep", "ctx", None),
            P("ep", "ctx", None),
            P("ep", "ctx", None),
            P("ep", "ctx", None),
            P("ep", "ctx", None),
            P("ep", "ctx", None),
            P("ep", "ctx", None),
        ),
        check_vma=False,
    )
```

profile of v0, /device:TPU:32, one launch (start us, length us, event | category | flops | bytes accessed | tf_op | source)
XLA Modules:
  0.0 645.9 jit_solution(3165984337473850861)
XLA Ops:
  9.8 31.3 %all-gather = bf16[1,1024,256]{1,2,0:T(8,128)(2,1)S(1)} all-gather(bf16[1,128,256]{1,2,0:T(8,128)(2,1)S(1)} %copy.75), channel_id=2, replica_groups=mesh['ctx'=8,'ep'=32] {'ctx'}, dimensions={1}, use_global_device_ids=true | all-gather | bytes 589824 | tf_op jit(solution)/shard_map/all_gather | solution.py:53
  42.6 22.0 %all-gather.1 = s32[1,1024]{1,0:T(1,128)S(1)} all-gather(s32[1,128]{1,0:T(1,128)} %param.15), channel_id=3, replica_groups=mesh['ctx'=8,'ep'=32] {'ctx'}, dimensions={1}, use_global_device_ids=true | all-gather | bytes 4608 | tf_op jit(solution)/shard_map/all_gather | solution.py:55
  64.7 35.0 %all-gather.2 = bf16[1,1024,256]{2,1,0:T(8,128)(2,1)S(1)} all-gather(bf16[1,128,256]{2,1,0:T(8,128)(2,1)} %param.14), channel_id=4, replica_groups=mesh['ctx'=8,'ep'=32] {'ctx'}, dimensions={1}, use_global_device_ids=true | all-gather | bytes 589824 | tf_op jit(solution)/shard_map/all_gather | solution.py:54
  100.2 4.9 fusion.69
  105.0 4.4 fusion.6
  109.5 2.0 bitcast_convert_fusion.3
  114.2 2.1 reshape.431
  118.1 5.4 scatter_custom_fusion
  123.5 2.4 reshape.391
  125.9 8.9 %all-to-all-start = ((bf16[32,20,2048]{2,1,0:T(8,128)(2,1)}), bf16[32,20,2048]{2,1,0:T(8,128)(2,1)}, u32[]{:S(2)}, u32[]{:S(2)}) async-start(bf16[32,20,2048]{2,1,0:T(8,128)(2,1)} %reshape.391), calls=%async_computation | async-start | bytes 6291456 | tf_op jit(solution)/shard_map/all_to_all | solution.py:32
  136.5 3.2 broadcast_in_dim.19
  139.7 5.3 convert_element_type.232
  145.2 6.1 scatter_custom_fusion.1
  151.3 2.3 reshape.397
  153.7 54.3 %all-to-all-done = bf16[32,20,2048]{2,1,0:T(8,128)(2,1)} async-done(((bf16[32,20,2048]{2,1,0:T(8,128)(2,1)}), bf16[32,20,2048]{2,1,0:T(8,128)(2,1)}, u32[]{:S(2)}, u32[]{:S(2)}) %all-to-all-start) | async-done | bytes 2621472 | tf_op jit(solution)/shard_map/all_to_all | solution.py:32
  207.9 4.6 all-to-all-start.2
  213.3 5.2 fusion.21
  218.5 58.1 %all-gather.7.cloned.1.call-done = bf16[1,2048,384]{2,1,0:T(8,128)(2,1)} async-done(((bf16[1,256,384]{2,1,0:T(8,128)(2,1)}), bf16[1,2048,384]{2,1,0:T(8,128)(2,1)}) %all-gather.7.cloned.1.call-update) | async-done | bytes 1572880 | tf_op jit(solution)/shard_map/all_gather | solution.py:89
  276.5 5.2 fusion.25
  281.7 49.6 %all-gather.11.cloned.1.call-done = bf16[1,2048,384]{2,1,0:T(8,128)(2,1)} async-done(((bf16[1,256,384]{2,1,0:T(8,128)(2,1)}), bf16[1,2048,384]{2,1,0:T(8,128)(2,1)}) %all-gather.11.cloned.1.call-update) | async-done | bytes 1572880 | tf_op jit(solution)/shard_map/all_gather | solution.py:91
  331.3 4.3 fusion.17
  335.6 2.8 fusion.60
  338.4 1.5 fusion.23
  341.5 3.2 copy.93
  344.7 7.8 %all-to-all-start.3 = ((bf16[32,20,2048]{2,1,0:T(8,128)(2,1)}), bf16[32,20,2048]{2,1,0:T(8,128)(2,1)}, u32[]{:S(2)}, u32[]{:S(2)}) async-start(bf16[32,20,2048]{2,1,0:T(8,128)(2,1)} %copy.93), calls=%async_computation.3 | async-start | bytes 6291456 | tf_op jit(solution)/shard_map/all_to_all | solution.py:32
  355.1 5.3 fusion.8
  360.4 65.1 %all-to-all-done.3 = bf16[32,20,2048]{2,1,0:T(8,128)(2,1)} async-done(((bf16[32,20,2048]{2,1,0:T(8,128)(2,1)}), bf16[32,20,2048]{2,1,0:T(8,128)(2,1)}, u32[]{:S(2)}, u32[]{:S(2)}) %all-to-all-start.3) | async-done | bytes 2621472 | tf_op jit(solution)/shard_map/all_to_all | solution.py:32
  425.6 3.6 reshape.400
  429.2 3.3 gather_fusion.1
  432.5 4.7 reshape.409
  437.3 4.9 reduce_sum.77
  444.1 2.7 fusion.44
  448.6 4.9 fusion.2
  453.5 2.1 copy-done.3
  458.7 4.1 fusion.9
  462.8 4.2 fusion.10
  467.0 2.5 pad_maximum_fusion
  470.8 1.6 convolution_convert_fusion
  472.4 3.1 copy.89
  475.5 5.1 all-to-all-start.1
  482.1 2.9 fusion.33
  486.0 67.5 %all-to-all-done.1 = bf16[32,20,2048]{2,1,0:T(8,128)(2,1)} async-done(((bf16[32,20,2048]{2,1,0:T(8,128)(2,1)}), bf16[32,20,2048]{2,1,0:T(8,128)(2,1)}, u32[]{:S(2)}, u32[]{:S(2)}) %all-to-all-start.1) | async-done | bytes 2621472 | tf_op jit(solution)/shard_map/all_to_all | solution.py:32
  553.5 3.8 reshape.396
  557.3 3.4 gather_fusion
  560.7 4.9 reshape.406
  565.6 2.7 multiply_reduce_fusion
  569.1 5.5 multiply_reduce_fusion.1
  577.6 57.7 %reduce-scatter.5.cloned.1.call-done = bf16[256,1152]{0,1:T(8,128)(2,1)} async-done(((bf16[2048,1152]{0,1:T(8,128)(2,1)}), bf16[256,1152]{0,1:T(8,128)(2,1)}) %reduce-scatter.5.cloned.1.call-update) | async-done | bytes 589840 | tf_op jit(solution)/shard_map/reduce_scatter | solution.py:114
  (127 shorter events, 33.6 us)
Async XLA Ops:
  7.2 92.8 %copy-start.31 = (s32[1,128]{1,0:T(1,128)S(1)}, s32[1,128]{1,0:T(1,128)}, u32[]{:S(2)}) copy-start(s32[1,128]{1,0:T(1,128)} %param.15) | copy-start | bytes 1540
  41.1 63.9 %copy-start.16 = (bf16[1,1024,256]{1,2,0:T(8,128)(2,1)}, bf16[1,1024,256]{1,2,0:T(8,128)(2,1)S(1)}, u32[]{:S(2)}) copy-start(bf16[1,1024,256]{1,2,0:T(8,128)(2,1)S(1)} %all-gather) | copy-start | bytes 1572868
  42.6 62.4 %copy-start.18 = (bf16[1,128,2048]{1,2,0:T(8,128)(2,1)}, bf16[1,128,2048]{1,2,0:T(8,128)(2,1)S(1)}, u32[]{:S(2)}) copy-start(bf16[1,128,2048]{1,2,0:T(8,128)(2,1)S(1)} %copy.142) | copy-start | bytes 1572868
  99.9 9.5 %copy-start.20 = (bf16[1,1024,256]{1,2,0:T(8,128)(2,1)}, bf16[1,1024,256]{1,2,0:T(8,128)(2,1)S(1)}, u32[]{:S(2)}) copy-start(bf16[1,1024,256]{1,2,0:T(8,128)(2,1)S(1)} %copy.78) | copy-start | bytes 1572868
  109.4 2.1 copy-start
  109.4 2.5 copy-start.9
  111.6 2.6 copy-start.6
  111.6 1.4 copy-start.29
  112.2 0.8 copy-start.12
  125.9 10.4 %copy-start.8 = (bf16[1,128,2048]{2,1,0:T(8,128)(2,1)S(1)}, bf16[1,128,2048]{2,1,0:T(8,128)(2,1)}, u32[]{:S(2)}) copy-start(bf16[1,128,2048]{2,1,0:T(8,128)(2,1)} %param.23) | copy-start | bytes 1572868
  125.9 82.0 %all-to-all-start = ((bf16[32,20,2048]{2,1,0:T(8,128)(2,1)}), bf16[32,20,2048]{2,1,0:T(8,128)(2,1)}, u32[]{:S(2)}, u32[]{:S(2)}) async-start(bf16[32,20,2048]{2,1,0:T(8,128)(2,1)} %reshape.391), calls=%async_computation | async-start | bytes 6291456 | tf_op jit(solution)/shard_map/all_to_all | solution.py:32
  134.9 78.4 %all-gather.9.cloned.1.call-start = ((), (), s32[]{:S(2)}) async-start(), calls=%async_computation.7 | async-start | bytes 1769472 | tf_op jit(solution)/shard_map/all_gather | solution.py:90
  135.6 140.9 %all-gather.7.cloned.1.call-start = ((), (), s32[]{:S(2)}) async-start(), calls=%async_computation.6 | async-start | bytes 1769472 | tf_op jit(solution)/shard_map/all_gather | solution.py:89
  139.7 5.3 copy-start.30
  207.9 123.4 %all-to-all-start.2 = ((bf16[32,20,2048]{2,1,0:T(8,128)(2,1)}), bf16[32,20,2048]{2,1,0:T(8,128)(2,1)}, u32[]{:S(2)}, u32[]{:S(2)}) async-start(bf16[32,20,2048]{2,1,0:T(8,128)(2,1)} %reshape.397), calls=%async_computation.2 | async-start | bytes 6291456 | tf_op jit(solution)/shard_map/all_to_all | solution.py:32
  212.5 118.8 %all-gather.11.cloned.1.call-start = ((), (), s32[]{:S(2)}) async-start(), calls=%async_computation.8 | async-start | bytes 1769472 | tf_op jit(solution)/shard_map/all_gather | solution.py:91
  331.3 4.3 copy-start.27
  335.6 2.8 copy-start.26
  338.4 1.6 copy-start.22
  338.4 1.6 copy-start.24
  344.7 9.2 %copy-start.10 = (bf16[1,128,2048]{2,1,0:T(8,128)(2,1)S(1)}, bf16[1,128,2048]{2,1,0:T(8,128)(2,1)}, u32[]{:S(2)}) copy-start(bf16[1,128,2048]{2,1,0:T(8,128)(2,1)} %param.16) | copy-start | bytes 1572868
  344.7 80.9 %all-to-all-start.3 = ((bf16[32,20,2048]{2,1,0:T(8,128)(2,1)}), bf16[32,20,2048]{2,1,0:T(8,128)(2,1)}, u32[]{:S(2)}, u32[]{:S(2)}) async-start(bf16[32,20,2048]{2,1,0:T(8,128)(2,1)} %copy.93), calls=%async_computation.3 | async-start | bytes 6291456 | tf_op jit(solution)/shard_map/all_to_all | solution.py:32
  352.6 223.5 %reduce-scatter.3.cloned.1.call-start = ((), (), s32[]{:S(2)}) async-start(), calls=%async_computation.9 | async-start | bytes 1179648 | tf_op jit(solution)/shard_map/reduce_scatter | solution.py:166
  437.2 6.2 copy-start.13
  442.1 4.7 copy-start.4
  442.2 2.0 copy-start.14
  443.5 3.3 copy-start.1
  446.8 1.7 copy-start.21
  448.6 7.0 %copy-start.19 = (bf16[1,128,2048]{1,2,0:T(8,128)(2,1)S(1)}, bf16[1,128,2048]{1,2,0:T(8,128)(2,1)}, u32[]{:S(2)}) copy-start(bf16[1,128,2048]{1,2,0:T(8,128)(2,1)} %copy-done.18) | copy-start | bytes 1572868
  453.5 2.1 copy-start.3
  457.1 1.6 copy-start.23
  458.4 4.4 copy-start.28
  458.4 176.9 %reduce-scatter.5.cloned.1.call-start = ((), (), s32[]{:S(2)}) async-start(), calls=%async_computation.10 | async-start | bytes 5308416 | tf_op jit(solution)/shard_map/reduce_scatter | solution.py:114
  462.8 4.2 copy-start.25
  469.4 1.4 copy-start.32
  475.5 5.2 copy-start.7
  475.5 6.5 %copy-start.17 = (bf16[1,1024,256]{1,2,0:T(8,128)(2,1)S(1)}, bf16[1,1024,256]{1,2,0:T(8,128)(2,1)}, u32[]{:S(2)}) copy-start(bf16[1,1024,256]{1,2,0:T(8,128)(2,1)} %copy-done.16) | copy-start | bytes 1572868
  475.5 77.9 %all-to-all-start.1 = ((bf16[32,20,2048]{2,1,0:T(8,128)(2,1)}), bf16[32,20,2048]{2,1,0:T(8,128)(2,1)}, u32[]{:S(2)}, u32[]{:S(2)}) async-start(bf16[32,20,2048]{2,1,0:T(8,128)(2,1)} %copy.89), calls=%async_computation.1 | async-start | bytes 6291456 | tf_op jit(solution)/shard_map/all_to_all | solution.py:32
  560.7 4.9 copy-start.2
  568.3 6.3 copy-start.5
  568.3 6.3 copy-start.11
  568.3 6.3 copy-start.15
Sparse Core Ops, SparseCore 0:
  138.3 65.5 all-gather.8
  206.5 69.9 all-gather.6
  279.1 52.1 all-gather.10
  458.5 77.0 reduce-scatter.2
  539.7 95.5 reduce-scatter.4
where the time goes:
time: 655 us; the launch traced here: 646 us
  waiting for transfers between devices  354 us (54%)
  blocking collectives  88.4 us (13%)
  local copies, waits for them, and re-layouts  73.9 us (11%)
  matrix products  50.5 us (8%)
  other arithmetic  37 us (6%)
  starting transfers between devices  27.6 us (4%)
  between operations  14.8 us (2%)
    all_to_all x4, waiting for transfers between devices, route_rows(): lax.all_to_all(rows.reshape(n_ep, -1, rows.shape[-1]), 'ep', split_axis=0...  187 us
    all_gather x1, waiting for transfers between devices, per_device(): lax.all_gather(w_gate, 'ctx', axis=1, tiled=True)  58.1 us
    reduce_scatter x1, waiting for transfers between devices, per_device(): lax.psum_scatter(jnp.stack([gate_term, up_term, down_term], axis=1).resha...  57.7 us
    all_gather x1, waiting for transfers between devices, per_device(): lax.all_gather(w_down, 'ctx', axis=1, tiled=True)  49.6 us
    all_gather x1, blocking collectives, per_device(): lax.all_gather(values[0], 'ctx', axis=0, tiled=True)  35 us
    all_gather x1, blocking collectives, per_device(): lax.all_gather(keys[0], 'ctx', axis=0, tiled=True)  31.3 us
    all_to_all x4, starting transfers between devices, route_rows(): lax.all_to_all(rows.reshape(n_ep, -1, rows.shape[-1]), 'ep', split_axis=0...  26.4 us
    all_gather x1, blocking collectives, per_device(): lax.all_gather(docs[0], 'ctx', axis=0, tiled=True)  22 us
  transfers between devices with their start and end apart: 9, of which 6 were waited for; matrix products, arithmetic and copies ran while one was open for 12% of the time, Pallas kernels for 0%

commit v1 on v0

--- a/solution.py
+++ b/solution.py
@@ -86,7 +86,9 @@
     )
     received = route_rows(outgoing, n_ep).reshape(n_ep, exp_dev, capacity, width)
     gate_full, up_full, down_full = (
-        lax.all_gather(w_gate, "ctx", axis=1, tiled=True),
+        jnp.concatenate(
+            lax.all_to_all(jnp.stack([w_gate] * lax.axis_size("ctx")), "ctx", 0, 0), axis=1
+        ),
         lax.all_gather(w_up, "ctx", axis=1, tiled=True),
         lax.all_gather(w_down, "ctx", axis=1, tiled=True),
     )

time: 655 us -> 624 us (0.953)
  waiting for transfers between devices: 354 us -> 307 us
  blocking collectives: 88.4 us -> 100 us
    all_gather x1 -> x0, waiting for transfers between devices: 58.1 us -> none  [per_device(): lax.all_gather(w_gate, 'ctx', axis=1, tiled=True)]
    all_gather x1, blocking collectives: 31.3 us -> 46.4 us  [per_device(): lax.all_gather(keys[0], 'ctx', axis=0, tiled=True)]
    all_gather x1, waiting for transfers between devices: 49.6 us -> 58.3 us  [per_device(): lax.all_gather(w_down, 'ctx', axis=1, tiled=True)]
    all_to_all x0 -> x1, starting transfers between devices: none -> 7.06 us  [per_device(): lax.all_to_all(jnp.stack([w_gate] * lax.axis_size('ctx')), 'ctx', 0, 0)]
  transfers between devices with their start and end apart: 9 -> 9, of which waited for: 6 -> 6; matrix products, arithmetic and copies ran while one was open for 12% -> 17% of each run, Pallas kernels for 0% -> 0%
where the time goes in v1:
time: 624 us; the launch traced here: 615 us
  waiting for transfers between devices  307 us (49%)
  blocking collectives  100 us (16%)
  local copies, waits for them, and re-layouts  71.7 us (11%)
  matrix products  51.9 us (8%)
  other arithmetic  36.4 us (6%)
  starting transfers between devices  32.4 us (5%)
  between operations  14.8 us (2%)
    all_to_all x4, waiting for transfers between devices, route_rows(): lax.all_to_all(rows.reshape(n_ep, -1, rows.shape[-1]), 'ep', split_axis=0...  191 us
    all_gather x1, waiting for transfers between devices, per_device(): lax.all_gather(w_down, 'ctx', axis=1, tiled=True)  58.3 us
    reduce_scatter x1, waiting for transfers between devices, per_device(): lax.psum_scatter(jnp.stack([gate_term, up_term, down_term], axis=1).resha...  57.2 us
    all_gather x1, blocking collectives, per_device(): lax.all_gather(keys[0], 'ctx', axis=0, tiled=True)  46.4 us
    all_gather x1, blocking collectives, per_device(): lax.all_gather(values[0], 'ctx', axis=0, tiled=True)  34.8 us
    all_to_all x4, starting transfers between devices, route_rows(): lax.all_to_all(rows.reshape(n_ep, -1, rows.shape[-1]), 'ep', split_axis=0...  24.2 us
    all_gather x1, blocking collectives, per_device(): lax.all_gather(docs[0], 'ctx', axis=0, tiled=True)  19 us
  transfers between devices with their start and end apart: 9, of which 6 were waited for; matrix products, arithmetic and copies ran while one was open for 17% of the time, Pallas kernels for 0%

profile of v1, /device:TPU:32, one launch (start us, length us, event | category | flops | bytes accessed | tf_op | source)
XLA Modules:
  0.0 614.9 jit_solution(14107199160909766770)
XLA Ops:
  7.2 2.3 stack.27
  9.5 7.1 %all-to-all-start.1 = ((bf16[8,1,256,384]{3,2,1,0:T(8,128)(2,1)}), bf16[8,1,256,384]{3,2,1,0:T(8,128)(2,1)}, u32[]{:S(2)}, u32[]{:S(2)}) async-start(bf16[8,1,256,384]{3,2,1,0:T(8,128)(2,1)} %stack.27), calls=%async_computation.1 | async-start | bytes 3145728 | tf_op jit(solution)/shard_map/all_to_all | solution.py:90
  17.0 46.4 %all-gather = bf16[1,1024,256]{1,2,0:T(8,128)(2,1)S(1)} all-gather(bf16[1,128,256]{1,2,0:T(8,128)(2,1)S(1)} %copy.75), channel_id=2, replica_groups=mesh['ctx'=8,'ep'=32] {'ctx'}, dimensions={1}, use_global_device_ids=true | all-gather | bytes 589824 | tf_op jit(solution)/shard_map/all_gather | solution.py:53
  63.7 19.0 %all-gather.1 = s32[1,1024]{1,0:T(1,128)S(1)} all-gather(s32[1,128]{1,0:T(1,128)S(1)} %copy-done.34), channel_id=3, replica_groups=mesh['ctx'=8,'ep'=32] {'ctx'}, dimensions={1}, use_global_device_ids=true | all-gather | bytes 4608 | tf_op jit(solution)/shard_map/all_gather | solution.py:55
  82.8 34.8 %all-gather.2 = bf16[1,1024,256]{2,1,0:T(8,128)(2,1)S(1)} all-gather(bf16[1,128,256]{2,1,0:T(8,128)(2,1)S(1)} %copy-done.30), channel_id=4, replica_groups=mesh['ctx'=8,'ep'=32] {'ctx'}, dimensions={1}, use_global_device_ids=true | all-gather | bytes 589824 | tf_op jit(solution)/shard_map/all_gather | solution.py:54
  118.0 4.8 fusion.66
  122.8 4.4 fusion.6
  127.2 2.0 bitcast_convert_fusion.3
  132.0 2.1 reshape.437
  135.9 5.4 scatter_custom_fusion
  141.3 2.4 reshape.397
  143.8 9.0 %all-to-all-start = ((bf16[32,20,2048]{2,1,0:T(8,128)(2,1)}), bf16[32,20,2048]{2,1,0:T(8,128)(2,1)}, u32[]{:S(2)}, u32[]{:S(2)}) async-start(bf16[32,20,2048]{2,1,0:T(8,128)(2,1)} %reshape.397), calls=%async_computation | async-start | bytes 6291456 | tf_op jit(solution)/shard_map/all_to_all | solution.py:32
  153.6 3.1 broadcast_in_dim.19
  156.7 5.3 convert_element_type.232
  162.3 6.1 scatter_custom_fusion.1
  168.4 2.4 reshape.403
  170.8 55.0 %all-to-all-done = bf16[32,20,2048]{2,1,0:T(8,128)(2,1)} async-done(((bf16[32,20,2048]{2,1,0:T(8,128)(2,1)}), bf16[32,20,2048]{2,1,0:T(8,128)(2,1)}, u32[]{:S(2)}, u32[]{:S(2)}) %all-to-all-start) | async-done | bytes 2621472 | tf_op jit(solution)/shard_map/all_to_all | solution.py:32
  225.8 4.6 all-to-all-start.3
  231.2 5.2 fusion.21
  236.4 5.2 fusion.67
  241.6 58.3 %all-gather.8.cloned.1.call-done = bf16[1,2048,384]{2,1,0:T(8,128)(2,1)} async-done(((bf16[1,256,384]{2,1,0:T(8,128)(2,1)}), bf16[1,2048,384]{2,1,0:T(8,128)(2,1)}) %all-gather.8.cloned.1.call-update) | async-done | bytes 1572880 | tf_op jit(solution)/shard_map/all_gather | solution.py:93
  299.9 3.4 all-to-all-done.3
  303.3 4.2 fusion.17
  307.6 2.7 fusion.56
  310.3 3.2 fusion.58
  315.0 3.3 copy.93
  318.3 5.5 all-to-all-start.4
  326.5 5.2 fusion.8
  331.7 65.2 %all-to-all-done.4 = bf16[32,20,2048]{2,1,0:T(8,128)(2,1)} async-done(((bf16[32,20,2048]{2,1,0:T(8,128)(2,1)}), bf16[32,20,2048]{2,1,0:T(8,128)(2,1)}, u32[]{:S(2)}, u32[]{:S(2)}) %all-to-all-start.4) | async-done | bytes 2621472 | tf_op jit(solution)/shard_map/all_to_all | solution.py:32
  396.9 3.6 reshape.406
  400.5 3.3 gather_fusion.1
  403.8 4.8 reshape.415
  408.6 4.9 reduce_sum.77
  415.5 2.7 fusion.40
  419.9 4.9 fusion.2
  428.3 4.1 fusion.9
  432.4 4.2 fusion.10
  436.6 2.5 pad_maximum_fusion
  442.1 3.1 copy.89
  445.2 5.1 all-to-all-start.2
  451.7 2.9 fusion.29
  455.6 67.4 %all-to-all-done.2 = bf16[32,20,2048]{2,1,0:T(8,128)(2,1)} async-done(((bf16[32,20,2048]{2,1,0:T(8,128)(2,1)}), bf16[32,20,2048]{2,1,0:T(8,128)(2,1)}, u32[]{:S(2)}, u32[]{:S(2)}) %all-to-all-start.2) | async-done | bytes 2621472 | tf_op jit(solution)/shard_map/all_to_all | solution.py:32
  523.1 3.7 reshape.402
  526.8 3.3 gather_fusion
  530.1 4.9 reshape.412
  535.0 2.7 multiply_reduce_fusion
  538.5 5.7 multiply_reduce_fusion.1
  547.2 57.2 %reduce-scatter.5.cloned.1.call-done = bf16[256,1152]{0,1:T(8,128)(2,1)} async-done(((bf16[2048,1152]{0,1:T(8,128)(2,1)}), bf16[256,1152]{0,1:T(8,128)(2,1)}) %reduce-scatter.5.cloned.1.call-update) | async-done | bytes 589840 | tf_op jit(solution)/shard_map/reduce_scatter | solution.py:116
  (133 shorter events, 31.5 us)
Async XLA Ops:
  7.2 9.4 %copy-start.33 = (s32[1,128,4]{1,2,0:T(4,128)S(1)}, s32[1,128,4]{1,2,0:T(4,128)}, u32[]{:S(2)}) copy-start(s32[1,128,4]{1,2,0:T(4,128)} %param.18) | copy-start | bytes 6148
  7.2 9.7 %copy-start.31 = (bf16[1,128,256]{2,1,0:T(8,128)(2,1)S(1)}, bf16[1,128,256]{2,1,0:T(8,128)(2,1)}, u32[]{:S(2)}) copy-start(bf16[1,128,256]{2,1,0:T(8,128)(2,1)} %param.13) | copy-start | bytes 196612
  7.2 56.2 %copy-start.27 = (bf16[1,128,2048]{2,1,0:T(8,128)(2,1)S(1)}, bf16[1,128,2048]{2,1,0:T(8,128)(2,1)}, u32[]{:S(2)}) copy-start(bf16[1,128,2048]{2,1,0:T(8,128)(2,1)} %param.12) | copy-start | bytes 1572868
  9.5 54.3 %copy-start.34 = (s32[1,128]{1,0:T(1,128)S(1)}, s32[1,128]{1,0:T(1,128)}, u32[]{:S(2)}) copy-start(s32[1,128]{1,0:T(1,128)} %param.15) | copy-start | bytes 1540
  9.5 73.3 %copy-start.30 = (bf16[1,128,256]{2,1,0:T(8,128)(2,1)S(1)}, bf16[1,128,256]{2,1,0:T(8,128)(2,1)}, u32[]{:S(2)}) copy-start(bf16[1,128,256]{2,1,0:T(8,128)(2,1)} %param.14) | copy-start | bytes 196612
  9.5 134.3 %all-to-all-start.1 = ((bf16[8,1,256,384]{3,2,1,0:T(8,128)(2,1)}), bf16[8,1,256,384]{3,2,1,0:T(8,128)(2,1)}, u32[]{:S(2)}, u32[]{:S(2)}) async-start(bf16[8,1,256,384]{3,2,1,0:T(8,128)(2,1)} %stack.27), calls=%async_computation.1 | async-start | bytes 3145728 | tf_op jit(solution)/shard_map/all_to_all | solution.py:90
  63.4 59.3 %copy-start.16 = (bf16[1,1024,256]{1,2,0:T(8,128)(2,1)}, bf16[1,1024,256]{1,2,0:T(8,128)(2,1)S(1)}, u32[]{:S(2)}) copy-start(bf16[1,1024,256]{1,2,0:T(8,128)(2,1)S(1)} %all-gather) | copy-start | bytes 1572868
  63.7 59.1 %copy-start.18 = (bf16[1,128,2048]{1,2,0:T(8,128)(2,1)}, bf16[1,128,2048]{1,2,0:T(8,128)(2,1)S(1)}, u32[]{:S(2)}) copy-start(bf16[1,128,2048]{1,2,0:T(8,128)(2,1)S(1)} %copy.142) | copy-start | bytes 1572868
  117.8 9.4 %copy-start.20 = (bf16[1,1024,256]{1,2,0:T(8,128)(2,1)}, bf16[1,1024,256]{1,2,0:T(8,128)(2,1)S(1)}, u32[]{:S(2)}) copy-start(bf16[1,1024,256]{1,2,0:T(8,128)(2,1)S(1)} %copy.78) | copy-start | bytes 1572868
  127.2 2.1 copy-start
  127.2 2.4 copy-start.9
  129.3 1.6 copy-start.6
  129.3 1.4 copy-start.29
  129.9 0.8 copy-start.12
  143.8 9.7 %copy-start.8 = (bf16[1,128,2048]{2,1,0:T(8,128)(2,1)S(1)}, bf16[1,128,2048]{2,1,0:T(8,128)(2,1)}, u32[]{:S(2)}) copy-start(bf16[1,128,2048]{2,1,0:T(8,128)(2,1)} %param.23) | copy-start | bytes 1572868
  143.8 82.0 %all-to-all-start = ((bf16[32,20,2048]{2,1,0:T(8,128)(2,1)}), bf16[32,20,2048]{2,1,0:T(8,128)(2,1)}, u32[]{:S(2)}, u32[]{:S(2)}) async-start(bf16[32,20,2048]{2,1,0:T(8,128)(2,1)} %reshape.397), calls=%async_computation | async-start | bytes 6291456 | tf_op jit(solution)/shard_map/all_to_all | solution.py:32
  152.8 78.4 %all-gather.6.cloned.1.call-start = ((), (), s32[]{:S(2)}) async-start(), calls=%async_computation.7 | async-start | bytes 1769472 | tf_op jit(solution)/shard_map/all_gather | solution.py:92
  156.7 5.3 copy-start.32
  225.8 77.5 %all-to-all-start.3 = ((bf16[32,20,2048]{2,1,0:T(8,128)(2,1)}), bf16[32,20,2048]{2,1,0:T(8,128)(2,1)}, u32[]{:S(2)}, u32[]{:S(2)}) async-start(bf16[32,20,2048]{2,1,0:T(8,128)(2,1)} %reshape.403), calls=%async_computation.3 | async-start | bytes 6291456 | tf_op jit(solution)/shard_map/all_to_all | solution.py:32
  230.4 69.5 %all-gather.8.cloned.1.call-start = ((), (), s32[]{:S(2)}) async-start(), calls=%async_computation.8 | async-start | bytes 1769472 | tf_op jit(solution)/shard_map/all_gather | solution.py:93
  303.3 4.3 copy-start.26
  310.3 3.2 copy-start.22
  310.3 3.2 copy-start.25
  318.3 7.0 %copy-start.10 = (bf16[1,128,2048]{2,1,0:T(8,128)(2,1)S(1)}, bf16[1,128,2048]{2,1,0:T(8,128)(2,1)}, u32[]{:S(2)}) copy-start(bf16[1,128,2048]{2,1,0:T(8,128)(2,1)} %param.16) | copy-start | bytes 1572868
  318.3 78.6 %all-to-all-start.4 = ((bf16[32,20,2048]{2,1,0:T(8,128)(2,1)}), bf16[32,20,2048]{2,1,0:T(8,128)(2,1)}, u32[]{:S(2)}, u32[]{:S(2)}) async-start(bf16[32,20,2048]{2,1,0:T(8,128)(2,1)} %copy.93), calls=%async_computation.4 | async-start | bytes 6291456 | tf_op jit(solution)/shard_map/all_to_all | solution.py:32
  323.8 221.8 %reduce-scatter.3.cloned.1.call-start = ((), (), s32[]{:S(2)}) async-start(), calls=%async_computation.9 | async-start | bytes 1179648 | tf_op jit(solution)/shard_map/reduce_scatter | solution.py:168
  408.6 6.2 %copy-start.13 = (bf16[128,2048]{1,0:T(8,128)(2,1)S(1)}, bf16[128,2048]{1,0:T(8,128)(2,1)}, u32[]{:S(2)}) copy-start(bf16[128,2048]{1,0:T(8,128)(2,1)} %copy-done.12) | copy-start | bytes 1572868
  413.5 4.7 copy-start.4
  413.5 2.0 copy-start.14
  414.8 3.3 copy-start.1
  418.2 1.7 copy-start.21
  419.9 4.9 copy-start.19
  424.8 1.9 copy-start.3
  426.8 1.6 copy-start.23
  428.1 4.3 copy-start.28
  428.1 176.3 %reduce-scatter.5.cloned.1.call-start = ((), (), s32[]{:S(2)}) async-start(), calls=%async_computation.10 | async-start | bytes 5308416 | tf_op jit(solution)/shard_map/reduce_scatter | solution.py:116
  432.4 4.2 copy-start.24
  439.1 1.4 copy-start.35
  445.2 5.2 copy-start.7
  445.2 6.5 %copy-start.17 = (bf16[1,1024,256]{1,2,0:T(8,128)(2,1)S(1)}, bf16[1,1024,256]{1,2,0:T(8,128)(2,1)}, u32[]{:S(2)}) copy-start(bf16[1,1024,256]{1,2,0:T(8,128)(2,1)} %copy-done.16) | copy-start | bytes 1572868
  445.2 77.9 %all-to-all-start.2 = ((bf16[32,20,2048]{2,1,0:T(8,128)(2,1)}), bf16[32,20,2048]{2,1,0:T(8,128)(2,1)}, u32[]{:S(2)}, u32[]{:S(2)}) async-start(bf16[32,20,2048]{2,1,0:T(8,128)(2,1)} %copy.89), calls=%async_computation.2 | async-start | bytes 6291456 | tf_op jit(solution)/shard_map/all_to_all | solution.py:32
  530.1 4.9 copy-start.2
  538.5 5.7 copy-start.5
  538.5 5.7 copy-start.11
  538.5 5.7 copy-start.15
Sparse Core Ops, SparseCore 0:
  156.1 66.1 all-gather.5
  233.8 66.0 all-gather.7
  428.2 76.5 reduce-scatter.2
  508.8 95.4 reduce-scatter.4
